TPU v7x, 32 devices: a whole 2x2x4 slice. The times are simulated.
32 devices in a mesh: row: 8 (over y, x, core), col: 4 (over z).
Axes of the slice: x: 2, y: 2, z: 4, core: 2. Of those that a mesh axis runs over, the one named last changes fastest.
Arguments:
- diag_factor: float32 [1024, 1024], P('row', 'col'), may hold values from -1 to 2.5, as said below
- panel_factor: float32 [4096, 1024], P('row', 'col'), may hold values from -0.09375 to 0.09375
- left_factor: float32 [4096, 2048], P('row', 'col'), may hold values from -0.09375 to 0.09375
- pivot_factor: float32 [1024, 2048], P('row', 'col'), may hold values from -0.1875 to 0.1875
- panel_adjoint: float32 [4096, 1024], P('row', 'col'), may hold values from -6 to 6
- left_adjoint: float32 [4096, 2048], P('row', 'col'), may hold values from -6 to 6
- pivot_adjoint: float32 [1024, 2048], P('row', 'col'), may hold values from -6 to 6
- diag_adjoint: float32 [1024, 1024], P('row', 'col'), may hold values from -6 to 6
Outputs:
- solved_panel: float32 [4096, 1024], P('row', 'col')
- left_out: float32 [4096, 2048], P('row', 'col')
- pivot_out: float32 [1024, 2048], P('row', 'col')
- diag_out: float32 [1024, 1024], P('row', 'col')
Inputs may be any that keep to these rules, and one draw needn't show every extreme that they name: diag_factor is lower triangular: zero above the diagonal, diagonal entries at least 1.
All inputs are finite; a program needn't handle non-finite values.
Results may differ from a plain program's by a relative error of at most 0.000073.
Values sent between devices are 32-bit elements; how exact they have to be, the bound alone decides.
No kernel may reach another device: no remote copies, remote signals or barrier semaphores. Data moves between devices by JAX's collectives and lax.ppermute only.
A program may use at most 64 MiB of HBM per device.

v0:
```python
import jax
import jax.numpy as jnp
from jax import lax
from jax.sharding import PartitionSpec as P


def right_solve(tile, source):
    return jax.scipy.linalg.solve_triangular(tile, source.T, trans="T", lower=True).T


def local(
    diag_factor,
    panel_factor,
    left_factor,
    pivot_factor,
    panel_adjoint,
    left_adjoint,
    pivot_adjoint,
    diag_adjoint,
):
    highest = lax.Precision.HIGHEST
    block_width = panel_adjoint.shape[1]
    my_col = lax.axis_index("col")
    my_row = lax.axis_index("row")
    column_block = lax.all_gather(diag_factor, "row", axis=0, tiled=True)
    whole_diag = lax.all_gather(column_block, "col", axis=1, tiled=True)
    full_rows = lax.all_gather(panel_adjoint, "col", axis=1, tiled=True)
    solved = right_solve(whole_diag, full_rows)
    solved_panel = lax.dynamic_slice_in_dim(solved, my_col * block_width, block_width, 1)
    picked = solved
    left_out = left_adjoint - jnp.dot(
        picked,
        lax.all_gather(pivot_factor, "row", axis=0, tiled=True),
        precision=highest,
        preferred_element_type=jnp.float32,
    )
    own_rows = diag_adjoint.shape[0]
    picked = solved
    square = jnp.einsum("rk,rc->kc", picked, panel_factor, precision=highest)
    pivot_part = jnp.einsum("rk,rc->kc", picked, left_factor, precision=highest)
    summed = lax.psum_scatter(
        jnp.concatenate([square, pivot_part], axis=1), "row", scatter_dimension=0, tiled=True
    )
    square_sum = summed[:, :block_width]
    pivot_sum = summed[:, block_width:]
    pivot_out = pivot_adjoint - pivot_sum
    global_row = my_row * own_rows + lax.broadcasted_iota(jnp.int32, (own_rows, block_width), 0)
    global_col = my_col * block_width + lax.broadcasted_iota(jnp.int32, (own_rows, block_width), 1)
    diag_out = diag_adjoint - jnp.where(global_col <= global_row, square_sum, 0.0)
    return (solved_panel, left_out, pivot_out, diag_out)


def solution(mesh):
    in_specs = (
        P("row", "col"),
        P("row", "col"),
        P("row", "col"),
        P("row", "col"),
        P("row", "col"),
        P("row", "col"),
        P("row", "col"),
        P("row", "col"),
    )
    out_specs = (P("row", "col"), P("row", "col"), P("row", "col"), P("row", "col"))
    return jax.shard_map(local, mesh=mesh, in_specs=in_specs, out_specs=out_specs, check_vma=False)
```

profile of v0, /device:TPU:0, one launch (start us, length us, event | category | flops | bytes accessed | tf_op | source)
XLA Modules:
  0.0 313.2 jit_solution(5399329404083906748)
XLA Ops:
  7.2 0.7 all-gather.5.cloned.1.call-update
  8.0 28.0 %all-gather.5.cloned.1.call-done = f32[1024,256]{1,0:T(8,128)} async-done(((f32[128,256]{1,0:T(8,128)}), f32[1024,256]{1,0:T(8,128)}) %all-gather.5.cloned.1.call-update) | async-done | bytes 1048592 | tf_op jit(solution)/shard_map/all_gather | solution.py:25
  36.1 0.7 all-gather.9.cloned.1.call-update
  36.8 0.5 all-gather.11.cloned.1.call-update
  37.4 80.9 %all-gather.7.cloned.1.call-done = f32[1024,1024]{1,0:T(8,128)} async-done(((f32[1024,256]{1,0:T(8,128)}), f32[1024,1024]{1,0:T(8,128)}) %all-gather.7.cloned.1.call-update) | async-done | bytes 4194320 | tf_op jit(solution)/shard_map/all_gather | solution.py:26
  118.3 4.8 %fusion = f32[1024,1024]{1,0:T(8,128)} fusion(f32[1024,1024]{1,0:T(8,128)} %all-gather.7.cloned.1.call-done), kind=kLoop, calls=%fused_computation.3 | loop fusion | flops 2097152 | bytes 8388608 | tf_op jit(solution)/shard_map/jit(_solve_triangular)/triangular_solve | solution.py:8
  123.1 23.2 %while.1 = (s32[]{:T(128)}, f32[1024,1024]{1,0:T(8,128)}, s32[8,2]{0,1:T(2,128)S(1)}, f32[8,128,128]{2,1,0:T(8,128)S(1)}, s32[]{:T(128)}) while((s32[]{:T(128)}, f32[1024,1024]{1,0:T(8,128)}, s32[8,2]{0,1:T(2,128)S(1)}, f32[8,128,128]{2,1,0:T(8,128)S(1)}, s32[]{:T(128)}) %tuple.27), condition=%wide.while_cond, body=%wide.while_body.sunk | while | flops 2 | bytes 131181 | solution.py:8
  123.2 0.5 fusion.56
  123.7 2.3 bitcast_dynamic-update-slice_fusion.2
  126.1 0.5 fusion.56
  126.6 2.3 bitcast_dynamic-update-slice_fusion.2
  129.0 0.5 fusion.56
  129.5 2.3 bitcast_dynamic-update-slice_fusion.2
  131.9 0.5 fusion.56
  132.4 2.3 bitcast_dynamic-update-slice_fusion.2
  134.8 0.5 fusion.56
  135.3 2.3 bitcast_dynamic-update-slice_fusion.2
  137.7 0.5 fusion.56
  138.3 2.3 bitcast_dynamic-update-slice_fusion.2
  140.6 0.5 fusion.56
  141.2 2.3 bitcast_dynamic-update-slice_fusion.2
  143.6 0.5 fusion.56
  144.1 2.2 bitcast_dynamic-update-slice_fusion.2
  146.3 78.8 %custom-call.4 = f32[8,128,128]{1,2,0:T(8,128)S(1)} custom-call(f32[8,128,128]{2,1,0:T(8,128)S(1)} %get-tuple-element.11), custom_call_target="InvertDiagBlocksLowerTriangular" | custom-call | tf_op jit(solution)/shard_map/jit(_solve_triangular)/triangular_solve | solution.py:8
  225.2 1.5 fusion.19
  226.7 1.6 convolution_subtract_fusion.4
  228.7 2.0 convolution_subtract_fusion.3
  231.1 2.4 convolution_subtract_fusion.6
  233.5 0.4 fusion.28
  233.9 2.8 convolution_subtract_fusion.7
  237.1 3.2 %convolution_subtract_fusion.2 = f32[128,512]{0,1:T(8,128)S(1)} fusion(f32[640,512]{1,0:T(8,128)S(1)} %constant_dynamic-update-slice_fusion, f32[1024,1024]{1,0:T(8,128)} %get-tuple-element.83, f32[1024,512]{0,1:T(8,128)S(1)} %bitcast.65), kind=kOutput, calls=%fused_computation.8 | convolution fusion | flops 503382016 | bytes 2162688 | tf_op jit(solution)/shard_map/jit(_solve_triangular)/triangular_solve | solution.py:8
  240.3 0.4 constant_dynamic-update-slice_fusion.10
  240.9 3.6 %convolution_subtract_fusion.5 = f32[128,512]{0,1:T(8,128)S(1)} fusion(f32[768,512]{1,0:T(8,128)S(1)} %constant_dynamic-update-slice_fusion.5, f32[1024,1024]{1,0:T(8,128)} %get-tuple-element.83, f32[1024,512]{0,1:T(8,128)S(1)} %bitcast.66), kind=kOutput, calls=%fused_computation.11 | convolution fusion | flops 604045312 | bytes 2490368 | tf_op jit(solution)/shard_map/jit(_solve_triangular)/triangular_solve | solution.py:8
  245.0 4.3 %convolution_subtract_fusion.1 = f32[128,512]{0,1:T(8,128)S(1)} fusion(f32[896,512]{1,0:T(8,128)S(1)} %constant_dynamic-update-slice_fusion.11, f32[1024,1024]{1,0:T(8,128)} %get-tuple-element.83, f32[1024,512]{0,1:T(8,128)S(1)} %bitcast.67), kind=kOutput, calls=%fused_computation.7 | convolution fusion | flops 704708608 | bytes 2818048 | tf_op jit(solution)/shard_map/jit(_solve_triangular)/triangular_solve | solution.py:8
  249.4 1.3 convolution_dynamic-update-slice_fusion
  250.8 2.0 fusion.36
  252.9 3.5 %fusion.37 = f32[1024,512]{0,1:T(8,128)S(1)} fusion(f32[1024,512]{1,0:T(8,128)S(1)} %constant_dynamic-update-slice_fusion.18, f32[512,512]{1,0:T(8,128)S(1)} %copy-done), kind=kOutput, calls=%fused_computation.89 | convolution fusion | flops 3221225472 | bytes 5242880 | tf_op jit(solution)/shard_map/rk,rc->kc/dot_general | solution.py:40
  256.4 2.0 pad_maximum_fusion
  258.5 1.1 copy.12
  259.5 1.0 copy.13
  260.6 0.8 dynamic-slice_bitcast_fusion
  261.4 2.1 copy.14
  263.5 6.6 %convolution_subtract_fusion = f32[512,512]{1,0:T(8,128)} fusion(f32[512,512]{1,0:T(8,128)} %param.13, f32[1024,512]{1,0:T(8,128)S(1)} %constant_dynamic-update-slice_fusion.18, f32[1024,512]{1,0:T(8,128)} %all-gather.11.cloned.1.call-done), kind=kOutput, calls=%fused_computation.5 | convolution fusion | flops 3221487616 | bytes 6291456 | tf_op jit(solution)/shard_map/dot_general | solution.py:31
  270.1 33.0 %reduce-scatter.2.cloned.1.call-done = f32[128,768]{0,1:T(8,128)} async-done(((f32[1024,768]{0,1:T(8,128)}), f32[128,768]{0,1:T(8,128)}) %reduce-scatter.2.cloned.1.call-update) | async-done | bytes 393232 | tf_op jit(solution)/shard_map/reduce_scatter | solution.py:41
  303.1 1.0 slice_subtract_fusion
  304.1 0.8 copy.15
  304.9 1.0 fusion.23
  305.9 0.8 copy.16
  (56 shorter events, 2.8 us)
Async XLA Ops:
  7.2 245.7 %copy-start = (f32[512,512]{1,0:T(8,128)S(1)}, f32[512,512]{1,0:T(8,128)}, u32[]{:S(2)}) copy-start(f32[512,512]{1,0:T(8,128)} %param.10) | copy-start | bytes 3145732
  7.2 28.8 %all-gather.5.cloned.1.call-start = ((), (), s32[]{:S(2)}) async-start(), calls=%async_computation.1 | async-start | bytes 1179648 | tf_op jit(solution)/shard_map/all_gather | solution.py:25
  7.9 110.4 %all-gather.7.cloned.1.call-start = ((), (), s32[]{:S(2)}) async-start(), calls=%async_computation.2 | async-start | bytes 5242880 | tf_op jit(solution)/shard_map/all_gather | solution.py:26
  36.0 189.1 %all-gather.9.cloned.1.call-start = ((), (), s32[]{:S(2)}) async-start(), calls=%async_computation.3 | async-start | bytes 2621440 | tf_op jit(solution)/shard_map/all_gather | solution.py:27
  36.8 226.7 %all-gather.11.cloned.1.call-start = ((), (), s32[]{:S(2)}) async-start(), calls=%async_computation.4 | async-start | bytes 2359296 | tf_op jit(solution)/shard_map/all_gather | solution.py:33
  37.3 265.8 %reduce-scatter.2.cloned.1.call-start = ((), (), s32[]{:S(2)}) async-start(), calls=%async_computation.5 | async-start | bytes 3538944 | tf_op jit(solution)/shard_map/reduce_scatter | solution.py:41
  225.1 19.4 %copy-start.3 = (f32[8,128,128]{1,2,0:T(8,128)}, f32[8,128,128]{1,2,0:T(8,128)S(1)}, u32[]{:S(2)}) copy-start(f32[8,128,128]{1,2,0:T(8,128)S(1)} %custom-call.4) | copy-start | bytes 1572868
  225.1 5.9 %copy-start.1 = (f32[512,1024]{1,0:T(8,128)S(1)}, f32[512,1024]{1,0:T(8,128)}, u32[]{:S(2)}) copy-start(f32[512,1024]{1,0:T(8,128)} %all-gather.9.cloned.1.call-done) | copy-start | bytes 6291460
  249.4 1.5 copy-start.2
Sparse Core Ops, SparseCore 0:
  9.9 26.0 all-gather.4
  37.6 80.7 all-gather.6
  119.9 44.1 all-gather.8
  165.9 26.7 all-gather.10
  258.6 44.4 reduce-scatter.1
where the time goes:
time: 314 us; the launch traced here: 313 us
  waiting for transfers between devices  144 us (46%)
  other arithmetic  87.5 us (28%)
  matrix products  37.1 us (12%)
  local copies, waits for them, and re-layouts  30.1 us (10%)
  between operations  14.2 us (5%)
    another operation x3, other arithmetic, right_solve(): jax.scipy.linalg.solve_triangular(tile, source.T, trans='T', lower=True)  83.5 us
    all_gather x1, waiting for transfers between devices, local(): whole_diag = lax.all_gather(column_block, 'col', axis=1, tiled=True)  80.9 us
    reduce_scatter x1, waiting for transfers between devices, local(): lax.psum_scatter(jnp.concatenate([square, pivot_part], axis=1), 'row', sc...  33 us
    all_gather x1, waiting for transfers between devices, local(): column_block = lax.all_gather(diag_factor, 'row', axis=0, tiled=True)  28 us
    another operation x15, matrix products, right_solve(): jax.scipy.linalg.solve_triangular(tile, source.T, trans='T', lower=True)  24.9 us
    another operation x24, local copies, waits for them, and re-layouts  23.1 us
    dot_general x1, matrix products, local(): jnp.dot(picked, lax.all_gather(pivot_factor, 'row', axis=0, tiled=True),...  6.61 us
  transfers between devices with their start and end apart: 5, of which 3 were waited for; matrix products, arithmetic and copies ran while one was open for 48% of the time, Pallas kernels for 0%

commit v1 on v0

--- a/solution.py
+++ b/solution.py
@@ -2,6 +2,19 @@
 import jax.numpy as jnp
 from jax import lax
 from jax.sharding import PartitionSpec as P
+
+
+def object_trace(field_in):
+    axis_tag = "col"
+    devs = jax.lax.axis_size(axis_tag)
+    inbox = [(i, (i + 1) % devs) for i in range(devs)]
+    r_now = [None] * devs
+    r_now[devs - 1] = field_in
+    for d in range(devs - 2, -1, -1):
+        r_now[d] = jax.lax.ppermute(r_now[d + 1], perm=inbox, axis_name=axis_tag)
+    tall = jnp.concatenate(r_now, axis=1)
+    low = (jax.lax.axis_index(axis_tag) + 1) * field_in.shape[1]
+    return jnp.roll(tall, low, 1)
 
 
 def right_solve(tile, source):
@@ -23,7 +36,7 @@
     my_col = lax.axis_index("col")
     my_row = lax.axis_index("row")
     column_block = lax.all_gather(diag_factor, "row", axis=0, tiled=True)
-    whole_diag = lax.all_gather(column_block, "col", axis=1, tiled=True)
+    whole_diag = object_trace(column_block)
     full_rows = lax.all_gather(panel_adjoint, "col", axis=1, tiled=True)
     solved = right_solve(whole_diag, full_rows)
     solved_panel = lax.dynamic_slice_in_dim(solved, my_col * block_width, block_width, 1)

time: 314 us -> 348 us (1.11)
  starting transfers between devices: 0.19 us -> 15.1 us
  waiting for transfers between devices: 144 us -> 155 us
  local copies, waits for them, and re-layouts: 30.1 us -> 39.7 us
    ppermute x0 -> x3, waiting for transfers between devices: none -> 94.4 us  [object_trace(): r_now[d] = jax.lax.ppermute(r_now[d + 1], perm=inbox, axis_name=axis_tag)]
    all_gather x1 -> x0, waiting for transfers between devices: 80.9 us -> none  [local(): whole_diag = lax.all_gather(column_block, 'col', axis=1, tiled=True)]
    ppermute x0 -> x3, starting transfers between devices: none -> 14.9 us  [object_trace(): r_now[d] = jax.lax.ppermute(r_now[d + 1], perm=inbox, axis_name=axis_tag)]
    another operation x24, local copies, waits for them, and re-layouts: 23.1 us -> 28.1 us
    unnamed x31 -> x40, local copies, waits for them, and re-layouts: 6.11 us -> 10.5 us
  transfers between devices with their start and end apart: 5 -> 7, of which waited for: 3 -> 5; matrix products, arithmetic and copies ran while one was open for 48% -> 46% of each run, Pallas kernels for 0% -> 0%
where the time goes in v1:
time: 348 us; the launch traced here: 347 us
  waiting for transfers between devices  155 us (45%)
  other arithmetic  86 us (25%)
  local copies, waits for them, and re-layouts  39.7 us (11%)
  matrix products  37 us (11%)
  starting transfers between devices  15.1 us (4%)
  between operations  14.3 us (4%)
    ppermute x3, waiting for transfers between devices, object_trace(): r_now[d] = jax.lax.ppermute(r_now[d + 1], perm=inbox, axis_name=axis_tag)  94.4 us
    another operation x3, other arithmetic, right_solve(): jax.scipy.linalg.solve_triangular(tile, source.T, trans='T', lower=True)  82 us
    reduce_scatter x1, waiting for transfers between devices, local(): lax.psum_scatter(jnp.concatenate([square, pivot_part], axis=1), 'row', sc...  32 us
    another operation x24, local copies, waits for them, and re-layouts  28.1 us
    all_gather x1, waiting for transfers between devices, local(): column_block = lax.all_gather(diag_factor, 'row', axis=0, tiled=True)  27.3 us
    another operation x15, matrix products, right_solve(): jax.scipy.linalg.solve_triangular(tile, source.T, trans='T', lower=True)  24.9 us
    ppermute x3, starting transfers between devices, object_trace(): r_now[d] = jax.lax.ppermute(r_now[d + 1], perm=inbox, axis_name=axis_tag)  14.9 us
    unnamed x40, local copies, waits for them, and re-layouts  10.5 us
  transfers between devices with their start and end apart: 7, of which 5 were waited for; matrix products, arithmetic and copies ran while one was open for 46% of the time, Pallas kernels for 0%

profile of v1, /device:TPU:0, one launch (start us, length us, event | category | flops | bytes accessed | tf_op | source)
XLA Modules:
  0.0 347.1 jit_solution(8311891098712543989)
XLA Ops:
  7.2 0.7 all-gather.4.cloned.1.call-update
  8.0 0.7 all-gather.6.cloned.1.call-update
  8.7 27.3 %all-gather.4.cloned.1.call-done = f32[1024,256]{1,0:T(8,128)} async-done(((f32[128,256]{1,0:T(8,128)}), f32[1024,256]{1,0:T(8,128)}) %all-gather.4.cloned.1.call-update) | async-done | bytes 1048592 | tf_op jit(solution)/shard_map/all_gather | solution.py:38
  36.0 1.5 collective-permute-start
  37.5 40.1 %collective-permute-done = f32[1024,256]{1,0:T(8,128)S(1)} collective-permute-done((f32[1024,256]{1,0:T(8,128)}, f32[1024,256]{1,0:T(8,128)S(1)}, u32[]{:S(2)}, u32[]{:S(2)}) %collective-permute-start) | collective-permute-done | bytes 1048608 | tf_op jit(solution)/shard_map/ppermute | solution.py:14
  77.6 13.4 %collective-permute-start.1 = (f32[1024,256]{1,0:T(8,128)S(1)}, f32[1024,256]{1,0:T(8,128)S(1)}, u32[]{:S(2)}, u32[]{:S(2)}) collective-permute-start(f32[1024,256]{1,0:T(8,128)S(1)} %collective-permute-done), channel_id=1, source_target_pairs={{0,1},{1,2},{2,3},{3,0},{4,5},{5,6},{6,7},{7,4},{8,9},{9,10},{10,1... | collective-permute-start | bytes 3145736 | tf_op jit(solution)/shard_map/ppermute | solution.py:14
  91.0 28.8 %collective-permute-done.1 = f32[1024,256]{1,0:T(8,128)S(1)} collective-permute-done((f32[1024,256]{1,0:T(8,128)S(1)}, f32[1024,256]{1,0:T(8,128)S(1)}, u32[]{:S(2)}, u32[]{:S(2)}) %collective-permute-start.1) | collective-permute-done | bytes 1048608 | tf_op jit(solution)/shard_map/ppermute | solution.py:14
  119.9 25.5 %collective-permute-done.2 = f32[1024,256]{1,0:T(8,128)} collective-permute-done((f32[1024,256]{1,0:T(8,128)S(1)}, f32[1024,256]{1,0:T(8,128)}, u32[]{:S(2)}, u32[]{:S(2)}) %collective-permute-start.2) | collective-permute-done | bytes 1048608 | tf_op jit(solution)/shard_map/ppermute | solution.py:14
  145.4 1.4 constant_dynamic-update-slice_fusion.7
  147.1 0.9 copy-done.1
  148.2 1.4 constant_dynamic-update-slice_fusion.3
  150.1 2.4 dynamic-slice_select_fusion
  152.5 28.1 %while.1 = (s32[]{:T(128)}, f32[1024,1024]{1,0:T(8,128)}, s32[8,2]{0,1:T(2,128)S(1)}, f32[8,128,128]{2,1,0:T(8,128)}, s32[]{:T(128)}) while((s32[]{:T(128)}, f32[1024,1024]{1,0:T(8,128)}, s32[8,2]{0,1:T(2,128)S(1)}, f32[8,128,128]{2,1,0:T(8,128)}, s32[]{:T(128)}) %tuple.27), condition=%wide.while_cond, body=%wide.while_body.sunk | while | flops 2 | bytes 132705 | solution.py:21
  152.6 0.5 fusion.55
  153.1 2.9 bitcast_dynamic-update-slice_fusion.2
  156.1 0.5 fusion.55
  156.6 2.9 bitcast_dynamic-update-slice_fusion.2
  159.6 0.5 fusion.55
  160.1 2.9 bitcast_dynamic-update-slice_fusion.2
  163.1 0.5 fusion.55
  163.7 2.9 bitcast_dynamic-update-slice_fusion.2
  167.2 2.9 bitcast_dynamic-update-slice_fusion.2
  170.7 2.9 bitcast_dynamic-update-slice_fusion.2
  174.2 2.9 bitcast_dynamic-update-slice_fusion.2
  177.7 2.9 bitcast_dynamic-update-slice_fusion.2
  180.6 79.6 %custom-call.4 = f32[8,128,128]{1,2,0:T(8,128)S(1)} custom-call(f32[8,128,128]{2,1,0:T(8,128)} %get-tuple-element.11), custom_call_target="InvertDiagBlocksLowerTriangular" | custom-call | tf_op jit(solution)/shard_map/jit(_solve_triangular)/triangular_solve | solution.py:21
  260.2 1.5 fusion.18
  261.8 1.6 convolution_subtract_fusion.4
  263.8 2.0 convolution_subtract_fusion.3
  266.2 2.4 convolution_subtract_fusion.6
  268.9 2.8 convolution_subtract_fusion.7
  272.2 3.2 convolution_subtract_fusion.2
  276.0 3.6 %convolution_subtract_fusion.5 = f32[128,512]{0,1:T(8,128)S(1)} fusion(f32[768,512]{1,0:T(8,128)S(1)} %constant_dynamic-update-slice_fusion.13, f32[1024,1024]{1,0:T(8,128)} %get-tuple-element.82, f32[1024,512]{0,1:T(8,128)S(1)} %bitcast.66), kind=kOutput, calls=%fused_computation.11 | convolution fusion | flops 604045312 | bytes 2490368 | tf_op jit(solution)/shard_map/jit(_solve_triangular)/triangular_solve | solution.py:21
  280.1 4.3 %convolution_subtract_fusion.1 = f32[128,512]{0,1:T(8,128)S(1)} fusion(f32[896,512]{1,0:T(8,128)S(1)} %constant_dynamic-update-slice_fusion.19, f32[1024,1024]{1,0:T(8,128)} %get-tuple-element.82, f32[1024,512]{0,1:T(8,128)S(1)} %bitcast.67), kind=kOutput, calls=%fused_computation.7 | convolution fusion | flops 704708608 | bytes 2818048 | tf_op jit(solution)/shard_map/jit(_solve_triangular)/triangular_solve | solution.py:21
  284.4 1.3 convolution_dynamic-update-slice_fusion
  285.9 2.0 fusion.35
  288.0 3.5 %fusion.36 = f32[1024,512]{0,1:T(8,128)S(1)} fusion(f32[1024,512]{1,0:T(8,128)S(1)} %constant_dynamic-update-slice_fusion.26, f32[512,512]{1,0:T(8,128)S(1)} %copy-done), kind=kOutput, calls=%fused_computation.97 | convolution fusion | flops 3221225472 | bytes 5242880 | tf_op jit(solution)/shard_map/rk,rc->kc/dot_general | solution.py:53
  291.5 2.0 pad_maximum_fusion
  293.5 1.1 copy.12
  294.6 1.0 copy.13
  295.7 0.8 dynamic-slice_bitcast_fusion
  296.5 2.0 copy.14
  298.5 6.5 %convolution_subtract_fusion = f32[512,512]{1,0:T(8,128)} fusion(f32[512,512]{1,0:T(8,128)} %param.13, f32[1024,512]{1,0:T(8,128)S(1)} %constant_dynamic-update-slice_fusion.26, f32[1024,512]{1,0:T(8,128)} %all-gather.8.cloned.1.call-done), kind=kOutput, calls=%fused_computation.5 | convolution fusion | flops 3221487616 | bytes 6291456 | tf_op jit(solution)/shard_map/dot_general | solution.py:44
  305.1 32.0 %reduce-scatter.2.cloned.1.call-done = f32[128,768]{0,1:T(8,128)} async-done(((f32[1024,768]{0,1:T(8,128)}), f32[128,768]{0,1:T(8,128)}) %reduce-scatter.2.cloned.1.call-update) | async-done | bytes 393232 | tf_op jit(solution)/shard_map/reduce_scatter | solution.py:54
  337.0 1.0 slice_subtract_fusion
  338.0 0.8 copy.15
  338.8 1.0 fusion.22
  339.9 0.8 copy.16
  (69 shorter events, 6.5 us)
Async XLA Ops:
  7.2 280.8 %copy-start = (f32[512,512]{1,0:T(8,128)S(1)}, f32[512,512]{1,0:T(8,128)}, u32[]{:S(2)}) copy-start(f32[512,512]{1,0:T(8,128)} %param.10) | copy-start | bytes 3145732
  7.2 28.8 %all-gather.4.cloned.1.call-start = ((), (), s32[]{:S(2)}) async-start(), calls=%async_computation.1 | async-start | bytes 1179648 | tf_op jit(solution)/shard_map/all_gather | solution.py:38
  7.9 252.3 %all-gather.6.cloned.1.call-start = ((), (), s32[]{:S(2)}) async-start(), calls=%async_computation.2 | async-start | bytes 2621440 | tf_op jit(solution)/shard_map/all_gather | solution.py:40
  8.7 289.9 %all-gather.8.cloned.1.call-start = ((), (), s32[]{:S(2)}) async-start(), calls=%async_computation.3 | async-start | bytes 2359296 | tf_op jit(solution)/shard_map/all_gather | solution.py:46
  36.0 41.6 %collective-permute-start = (f32[1024,256]{1,0:T(8,128)}, f32[1024,256]{1,0:T(8,128)S(1)}, u32[]{:S(2)}, u32[]{:S(2)}) collective-permute-start(f32[1024,256]{1,0:T(8,128)} %all-gather.4.cloned.1.call-done), channel_id=1, source_target_pairs={{0,1},{1,2},{2,3},{3,0},{4,5},{5,6},{6,7},{7,4},{8,9},{9,10},{10,1... | collective-permute-start | bytes 3145736 | tf_op jit(solution)/shard_map/ppermute | solution.py:14
  77.6 42.2 %collective-permute-start.1 = (f32[1024,256]{1,0:T(8,128)S(1)}, f32[1024,256]{1,0:T(8,128)S(1)}, u32[]{:S(2)}, u32[]{:S(2)}) collective-permute-start(f32[1024,256]{1,0:T(8,128)S(1)} %collective-permute-done), channel_id=1, source_target_pairs={{0,1},{1,2},{2,3},{3,0},{4,5},{5,6},{6,7},{7,4},{8,9},{9,10},{10,1... | collective-permute-start | bytes 3145736 | tf_op jit(solution)/shard_map/ppermute | solution.py:14
  119.8 25.6 %collective-permute-start.2 = (f32[1024,256]{1,0:T(8,128)S(1)}, f32[1024,256]{1,0:T(8,128)}, u32[]{:S(2)}, u32[]{:S(2)}) collective-permute-start(f32[1024,256]{1,0:T(8,128)S(1)} %collective-permute-done.1), channel_id=1, source_target_pairs={{0,1},{1,2},{2,3},{3,0},{4,5},{5,6},{6,7},{7,4},{8,9},{9,10},{10,1... | collective-permute-start | bytes 3145736 | tf_op jit(solution)/shard_map/ppermute | solution.py:14
  119.8 217.2 %reduce-scatter.2.cloned.1.call-start = ((), (), s32[]{:S(2)}) async-start(), calls=%async_computation.4 | async-start | bytes 3538944 | tf_op jit(solution)/shard_map/reduce_scatter | solution.py:54
  146.8 1.3 copy-start.1
  260.2 19.4 %copy-start.4 = (f32[8,128,128]{1,2,0:T(8,128)}, f32[8,128,128]{1,2,0:T(8,128)S(1)}, u32[]{:S(2)}) copy-start(f32[8,128,128]{1,2,0:T(8,128)S(1)} %custom-call.4) | copy-start | bytes 1572868
  260.2 5.9 %copy-start.2 = (f32[512,1024]{1,0:T(8,128)S(1)}, f32[512,1024]{1,0:T(8,128)}, u32[]{:S(2)}) copy-start(f32[512,1024]{1,0:T(8,128)} %all-gather.6.cloned.1.call-done) | copy-start | bytes 6291460
  284.4 1.5 copy-start.3
Sparse Core Ops, SparseCore 0:
  9.9 26.0 all-gather.3
  37.6 63.3 all-gather.5
  119.9 28.2 all-gather.7
  293.7 43.3 reduce-scatter.1
